TPU v7x, 512 devices: a whole 4x4x16 slice. The times are simulated.
512 devices in a mesh: dp: 4 (over x), mp: 128 (over z, y, core).
Axes of the slice: x: 4, y: 4, z: 16, core: 2. Of those that a mesh axis runs over, the one named last changes fastest.
Arguments:
- acts: bfloat16 [8192, 16384], P('dp', 'mp'), may hold values from -6 to 6
- diag_weight: bfloat16 [7, 16384, 128], P(None, 'mp'), may hold values from -0.375 to 0.375
- cross_weight: bfloat16 [7, 16384, 128], P(None, 'mp'), may hold values from -0.375 to 0.375
- low_in: bfloat16 [16384, 64], P('mp'), may hold values from -0.046875 to 0.046875
- low_out: bfloat16 [64, 16384], P(None, 'mp'), may hold values from -0.75 to 0.75
- cotangent: bfloat16 [8192, 16384], P('dp', 'mp'), may hold values from -6 to 6
Outputs:
- output: bfloat16 [8192, 16384], P('dp', 'mp')
- grad_acts: bfloat16 [8192, 16384], P('dp', 'mp')
- grad_diag: float32 [7, 16384, 128], P(None, 'mp')
- grad_cross: float32 [7, 16384, 128], P(None, 'mp')
- grad_low_in: float32 [16384, 64], P('mp')
- grad_low_out: float32 [64, 16384], P(None, 'mp')
All inputs are finite; a program needn't handle non-finite values.
Results may differ from a plain program's by a relative error of at most 0.019.
Values may be sent and summed in bfloat16 or wider, within the bound.
A program may use at most 64 MiB of HBM per device.

v0:
```python
import jax
import jax.numpy as jnp
from jax import lax
from jax.sharding import PartitionSpec as P


def swapped(block, axis, stride):
    count = lax.axis_size(axis)
    route = []
    for low in range(count):
        high = low | 1 << stride
        if high != low and high < count:
            route += [(low, high), (high, low)]
    return lax.ppermute(block, axis, route)


def gelu_slope(pre, cot):
    return jax.vjp(lambda v: jax.nn.gelu(v, approximate=True), pre)[1](cot)[0]


def rank_total(acts, low_in):
    partial_low = jnp.dot(acts, low_in, preferred_element_type=jnp.float32)
    return lax.psum(partial_low, "mp")


def per_device(acts, diag_weight, cross_weight, low_in, low_out, cotangent):
    sections = lax.axis_size("mp").bit_length() - 1
    scale = float(acts.shape[0] * lax.axis_size("dp")) ** (-0.5)
    low = None
    state = acts
    saved = []
    partners = []
    mixed = None
    for section in range(sections):
        other = swapped(state, "mp", section)
        saved.append(state)
        partners.append(other)
        fresh = jnp.dot(state, diag_weight[section], preferred_element_type=jnp.float32)
        fresh = fresh + jnp.dot(other, cross_weight[section], preferred_element_type=jnp.float32)
        if section < sections - 1:
            state = fresh.astype(jnp.bfloat16)
        else:
            mixed = fresh
    low = rank_total(acts, low_in)
    low_b = low.astype(jnp.bfloat16)
    pre = mixed + jnp.dot(low_b, low_out, preferred_element_type=jnp.float32)
    output = jax.nn.gelu(pre, approximate=True).astype(jnp.bfloat16)
    d_pre = gelu_slope(pre, cotangent.astype(jnp.float32)).astype(jnp.bfloat16)
    partial_back = jnp.dot(d_pre, low_out.T, preferred_element_type=jnp.float32)
    d_low = lax.psum(partial_back, "mp").astype(jnp.bfloat16)
    low_back = jnp.dot(d_low, low_in.T, preferred_element_type=jnp.float32)
    local_in = scale * jnp.dot(acts.T, d_low, preferred_element_type=jnp.float32)
    local_out = scale * jnp.dot(low_b.T, d_pre, preferred_element_type=jnp.float32)
    grad_low_in, grad_low_out = (
        lax.psum(local_in.astype(jnp.bfloat16), "dp").astype(jnp.float32),
        lax.psum(local_out.astype(jnp.bfloat16), "dp").astype(jnp.float32),
    )
    upper = d_pre
    grads_d = [None] * sections
    grads_c = [None] * sections
    grad_acts = None
    for section in range(sections - 1, -1, -1):
        term_d = scale * jnp.dot(saved[section].T, upper, preferred_element_type=jnp.float32)
        term_c = scale * jnp.dot(partners[section].T, upper, preferred_element_type=jnp.float32)
        term_d, term_c = (
            lax.psum(term_d.astype(jnp.bfloat16), "dp").astype(jnp.float32),
            lax.psum(term_c.astype(jnp.bfloat16), "dp").astype(jnp.float32),
        )
        grads_d[section] = term_d
        grads_c[section] = term_c
        sent = jnp.dot(upper, cross_weight[section].T, preferred_element_type=jnp.float32).astype(
            jnp.bfloat16
        )
        arrived = swapped(sent, "mp", section)
        back = jnp.dot(
            upper, diag_weight[section].T, preferred_element_type=jnp.float32
        ) + arrived.astype(jnp.float32)
        if section > 0:
            upper = back.astype(jnp.bfloat16)
        else:
            grad_acts = (back + low_back).astype(jnp.bfloat16)
    grad_diag = jnp.stack(grads_d)
    grad_cross = jnp.stack(grads_c)
    return (output, grad_acts, grad_diag, grad_cross, grad_low_in, grad_low_out)


def solution(mesh):
    placed = (
        P("dp", "mp"),
        P(None, "mp", None),
        P(None, "mp", None),
        P("mp", None),
        P(None, "mp"),
        P("dp", "mp"),
    )
    return jax.shard_map(
        per_device,
        mesh=mesh,
        in_specs=placed,
        out_specs=(
            P("dp", "mp"),
            P("dp", "mp"),
            P(None, "mp", None),
            P(None, "mp", None),
            P("mp", None),
            P(None, "mp"),
        ),
        check_vma=False,
    )
```

profile of v0, /device:TPU:8, one launch (start us, length us, event | category | flops | bytes accessed | tf_op | source)
XLA Modules:
  0.0 1379.5 jit_solution(5612966932018341492)
XLA Ops:
  7.2 2.1 collective-permute-start
  9.3 1.3 fusion.95
  12.2 7.7 collective-permute-start.1
  20.2 11.9 collective-permute-done.1
  32.9 1.9 collective-permute-start.2
  35.1 14.6 %collective-permute-done.2 = bf16[2048,128]{1,0:T(8,128)(2,1)S(1)} collective-permute-done((bf16[2048,128]{1,0:T(8,128)(2,1)S(1)}, bf16[2048,128]{1,0:T(8,128)(2,1)S(1)}, u32[]{:S(2)}, u32[]{:S(2)}) %collective-permute-start.2) | collective-permute-done | bytes 524320 | tf_op jit(solution)/shard_map/ppermute | solution.py:14
  50.6 1.9 collective-permute-start.3
  52.8 12.2 collective-permute-done.3
  65.8 1.9 collective-permute-start.4
  68.0 23.4 %collective-permute-done.4 = bf16[2048,128]{1,0:T(8,128)(2,1)S(1)} collective-permute-done((bf16[2048,128]{1,0:T(8,128)(2,1)S(1)}, bf16[2048,128]{1,0:T(8,128)(2,1)S(1)}, u32[]{:S(2)}, u32[]{:S(2)}) %collective-permute-start.4) | collective-permute-done | bytes 524320 | tf_op jit(solution)/shard_map/ppermute | solution.py:14
  92.2 5.0 collective-permute-start.5
  97.9 45.3 %collective-permute-done.5 = bf16[2048,128]{1,0:T(8,128)(2,1)S(1)} collective-permute-done((bf16[2048,128]{1,0:T(8,128)(2,1)S(1)}, bf16[2048,128]{1,0:T(8,128)(2,1)S(1)}, u32[]{:S(2)}, u32[]{:S(2)}) %collective-permute-start.5) | collective-permute-done | bytes 524320 | tf_op jit(solution)/shard_map/ppermute | solution.py:14
  144.0 22.4 %collective-permute-start.6 = (bf16[2048,128]{1,0:T(8,128)(2,1)S(1)}, bf16[2048,128]{1,0:T(8,128)(2,1)S(1)}, u32[]{:S(2)}, u32[]{:S(2)}) collective-permute-start(bf16[2048,128]{1,0:T(8,128)(2,1)S(1)} %fusion.6), channel_id=1, source_target_pairs={{0,64},{64,0},{1,65},{65,1},{2,66},{66,2},{3,67},{67,3},{4,68},{68... | collective-permute-start | bytes 1572872 | tf_op jit(solution)/shard_map/ppermute | solution.py:14
  166.4 497.5 %all-reduce.6 = bf16[2048,64]{0,1:T(8,128)(2,1)S(1)} all-reduce(f32[2048,64]{0,1:T(8,128)S(1)} %fusion.125), channel_id=1, replica_groups=mesh['dp'=4,'mp'=128] {'mp'}, use_global_device_ids=true, to_apply=%region_0.0 | all-reduce | flops 131072 | bytes 786432 | tf_op jit(solution)/shard_map/psum | solution.py:23
  663.9 1.1 fusion.63
  666.3 1.9 fusion.46
  668.4 30.1 %collective-permute-start.7 = (bf16[2048,128]{1,0:T(8,128)(2,1)S(1)}, bf16[2048,128]{1,0:T(8,128)(2,1)S(1)}, u32[]{:S(2)}, u32[]{:S(2)}) collective-permute-start(bf16[2048,128]{1,0:T(8,128)(2,1)S(1)} %convolution_convert_fusion.6), channel_id=1, source_target_pairs={{0,64},{64,0},{1,65},{65,1},{2,66},{66,2},{3,67},{67,3},{4,68},{68... | collective-permute-start | bytes 1572872 | tf_op jit(solution)/shard_map/ppermute | solution.py:14
  698.5 9.3 collective-permute-done.7
  707.9 1.1 add_convert_fusion
  709.2 1.9 collective-permute-start.8
  711.1 1.1 fusion.126
  712.2 37.0 %collective-permute-done.8 = bf16[2048,128]{1,0:T(8,128)(2,1)S(1)} collective-permute-done((bf16[2048,128]{1,0:T(8,128)(2,1)S(1)}, bf16[2048,128]{1,0:T(8,128)(2,1)S(1)}, u32[]{:S(2)}, u32[]{:S(2)}) %collective-permute-start.8) | collective-permute-done | bytes 524320 | tf_op jit(solution)/shard_map/ppermute | solution.py:14
  749.3 1.1 fusion.7
  750.3 1.1 convolution_convert_fusion.4
  751.4 1.9 collective-permute-start.9
  754.2 491.6 %all-reduce.7 = bf16[2048,64]{0,1:T(8,128)(2,1)S(1)} all-reduce(f32[2048,64]{0,1:T(8,128)} %fusion.126), channel_id=1, replica_groups=mesh['dp'=4,'mp'=128] {'mp'}, use_global_device_ids=true, to_apply=%region_1.0 | all-reduce | flops 131072 | bytes 786432 | tf_op jit(solution)/shard_map/psum | solution.py:50
  1246.7 1.3 fusion.8
  1248.0 1.1 convolution_convert_fusion.3
  1249.2 2.1 collective-permute-start.10
  1251.2 1.0 fusion.34
  1252.2 1.0 fusion.27
  1255.3 5.1 collective-permute-done.10
  1260.7 1.1 convolution_convert_fusion.2
  1261.8 2.1 collective-permute-start.11
  1263.9 1.0 fusion.36
  1265.9 1.0 fusion.37
  1267.0 1.0 fusion.30
  1267.9 6.6 collective-permute-done.11
  1274.8 1.1 convolution_convert_fusion.1
  1275.9 10.6 collective-permute-start.12
  1286.5 1.0 fusion.38
  1288.4 1.0 fusion.39
  1290.4 3.0 collective-permute-done.12
  1296.1 1.1 convolution_convert_fusion
  1297.2 1.9 collective-permute-start.13
  1299.1 58.6 %all-reduce.5.cloned.1.call-done = (bf16[1,128,128]{1,2,0:T(8,128)(2,1)}, bf16[1,128,128]{1,2,0:T(8,128)(2,1)}, bf16[1,128,128]{1,2,0:T(8,128)(2,1)}, bf16[1,128...) async-done(((bf16[1,128,128]{1,2,0:T(8,128)(2,1)}, ...) | async-done | bytes 491536 | tf_op jit(solution)/shard_map/psum | solution.py:66
  1357.8 1.3 convert_element_type.223
  1370.8 1.8 fusion.12
  (140 shorter events, 30.9 us)
Async XLA Ops:
  7.2 658.7 %copy-start = (bf16[64,128]{1,0:T(8,128)(2,1)S(1)}, bf16[64,128]{1,0:T(8,128)(2,1)}, u32[]{:S(2)}) copy-start(bf16[64,128]{1,0:T(8,128)(2,1)} %param.10) | copy-start | bytes 49156
  7.2 4.2 copy-start.24
  7.2 1350.6 %all-reduce.5.cloned.1.call-start = ((), (), s32[]{:S(2)}) async-start(), calls=%async_computation | async-start | bytes 983040 | tf_op jit(solution)/shard_map/psum | solution.py:66
  7.2 4.1 collective-permute-start
  10.6 9.3 copy-start.26
  11.4 0.8 copy-start.10
  12.2 19.9 %collective-permute-start.1 = (bf16[2048,128]{1,0:T(8,128)(2,1)S(1)}, bf16[2048,128]{1,0:T(8,128)(2,1)S(1)}, u32[]{:S(2)}, u32[]{:S(2)}) collective-permute-start(bf16[2048,128]{1,0:T(8,128)(2,1)S(1)} %fusion.1), channel_id=1, source_target_pairs={{0,2},{2,0},{1,3},{3,1},{4,6},{6,4},{5,7},{7,5},{8,10},{10,8},{9,1... | collective-permute-start | bytes 1572872 | tf_op jit(solution)/shard_map/ppermute | solution.py:14
  32.1 0.8 copy-start.12
  32.9 16.8 %collective-permute-start.2 = (bf16[2048,128]{1,0:T(8,128)(2,1)S(1)}, bf16[2048,128]{1,0:T(8,128)(2,1)S(1)}, u32[]{:S(2)}, u32[]{:S(2)}) collective-permute-start(bf16[2048,128]{1,0:T(8,128)(2,1)S(1)} %fusion.2), channel_id=1, source_target_pairs={{0,4},{4,0},{1,5},{5,1},{2,6},{6,2},{3,7},{7,3},{8,12},{12,8},{9,1... | collective-permute-start | bytes 1572872 | tf_op jit(solution)/shard_map/ppermute | solution.py:14
  49.8 0.8 copy-start.14
  50.6 2.2 copy-start.2
  50.6 14.4 %collective-permute-start.3 = (bf16[2048,128]{1,0:T(8,128)(2,1)S(1)}, bf16[2048,128]{1,0:T(8,128)(2,1)S(1)}, u32[]{:S(2)}, u32[]{:S(2)}) collective-permute-start(bf16[2048,128]{1,0:T(8,128)(2,1)S(1)} %fusion.3), channel_id=1, source_target_pairs={{0,8},{8,0},{1,9},{9,1},{2,10},{10,2},{3,11},{11,3},{4,12},{12,4},... | collective-permute-start | bytes 1572872 | tf_op jit(solution)/shard_map/ppermute | solution.py:14
  65.0 0.8 copy-start.16
  65.8 2.2 copy-start.4
  65.8 25.6 %collective-permute-start.4 = (bf16[2048,128]{1,0:T(8,128)(2,1)S(1)}, bf16[2048,128]{1,0:T(8,128)(2,1)S(1)}, u32[]{:S(2)}, u32[]{:S(2)}) collective-permute-start(bf16[2048,128]{1,0:T(8,128)(2,1)S(1)} %fusion.4), channel_id=1, source_target_pairs={{0,16},{16,0},{1,17},{17,1},{2,18},{18,2},{3,19},{19,3},{4,20},{20... | collective-permute-start | bytes 1572872 | tf_op jit(solution)/shard_map/ppermute | solution.py:14
  68.0 29.2 %copy-start.1 = (bf16[2048,128]{1,0:T(8,128)(2,1)S(1)}, bf16[2048,128]{1,0:T(8,128)(2,1)}, u32[]{:S(2)}) copy-start(bf16[2048,128]{1,0:T(8,128)(2,1)} %param.6) | copy-start | bytes 1572868
  68.0 29.2 %copy-start.28 = (bf16[128,64]{0,1:T(8,128)(2,1)S(1)}, bf16[128,64]{0,1:T(8,128)(2,1)}, u32[]{:S(2)}) copy-start(bf16[128,64]{0,1:T(8,128)(2,1)} %param.9) | copy-start | bytes 49156
  91.5 0.8 copy-start.18
  92.2 5.3 copy-start.6
  92.2 51.0 %collective-permute-start.5 = (bf16[2048,128]{1,0:T(8,128)(2,1)S(1)}, bf16[2048,128]{1,0:T(8,128)(2,1)S(1)}, u32[]{:S(2)}, u32[]{:S(2)}) collective-permute-start(bf16[2048,128]{1,0:T(8,128)(2,1)S(1)} %fusion.5), channel_id=1, source_target_pairs={{0,32},{32,0},{1,33},{33,1},{2,34},{34,2},{3,35},{35,3},{4,36},{36... | collective-permute-start | bytes 1572872 | tf_op jit(solution)/shard_map/ppermute | solution.py:14
  143.2 0.8 copy-start.20
  144.0 521.0 %copy-start.8 = (bf16[2048,128]{1,0:T(8,128)(2,1)}, bf16[2048,128]{1,0:T(8,128)(2,1)S(1)}, u32[]{:S(2)}) copy-start(bf16[2048,128]{1,0:T(8,128)(2,1)S(1)} %fusion.6) | copy-start | bytes 1572868
  144.0 521.0 %collective-permute-start.6 = (bf16[2048,128]{1,0:T(8,128)(2,1)S(1)}, bf16[2048,128]{1,0:T(8,128)(2,1)S(1)}, u32[]{:S(2)}, u32[]{:S(2)}) collective-permute-start(bf16[2048,128]{1,0:T(8,128)(2,1)S(1)} %fusion.6), channel_id=1, source_target_pairs={{0,64},{64,0},{1,65},{65,1},{2,66},{66,2},{3,67},{67,3},{4,68},{68... | collective-permute-start | bytes 1572872 | tf_op jit(solution)/shard_map/ppermute | solution.py:14
  663.9 1.1 copy-start.25
  665.0 1.2 copy-start.44
  665.1 0.8 copy-start.22
  668.4 39.4 %collective-permute-start.7 = (bf16[2048,128]{1,0:T(8,128)(2,1)S(1)}, bf16[2048,128]{1,0:T(8,128)(2,1)S(1)}, u32[]{:S(2)}, u32[]{:S(2)}) collective-permute-start(bf16[2048,128]{1,0:T(8,128)(2,1)S(1)} %convolution_convert_fusion.6), channel_id=1, source_target_pairs={{0,64},{64,0},{1,65},{65,1},{2,66},{66,2},{3,67},{67,3},{4,68},{68... | collective-permute-start | bytes 1572872 | tf_op jit(solution)/shard_map/ppermute | solution.py:14
  709.2 40.1 %collective-permute-start.8 = (bf16[2048,128]{1,0:T(8,128)(2,1)S(1)}, bf16[2048,128]{1,0:T(8,128)(2,1)S(1)}, u32[]{:S(2)}, u32[]{:S(2)}) collective-permute-start(bf16[2048,128]{1,0:T(8,128)(2,1)S(1)} %convolution_convert_fusion.5), channel_id=1, source_target_pairs={{0,32},{32,0},{1,33},{33,1},{2,34},{34,2},{3,35},{35,3},{4,36},{36... | collective-permute-start | bytes 1572872 | tf_op jit(solution)/shard_map/ppermute | solution.py:14
  751.4 495.1 %collective-permute-start.9 = (bf16[2048,128]{1,0:T(8,128)(2,1)}, bf16[2048,128]{1,0:T(8,128)(2,1)}, u32[]{:S(2)}, u32[]{:S(2)}) collective-permute-start(bf16[2048,128]{1,0:T(8,128)(2,1)} %convolution_convert_fusion.4), channel_id=1, source_target_pairs={{0,16},{16,0},{1,17},{17,1},{2,18},{18,2},{3,19},{19,3},{4,20},{20... | collective-permute-start | bytes 1572872 | tf_op jit(solution)/shard_map/ppermute | solution.py:14
  1245.8 0.9 copy-start.27
  1248.0 3.2 copy-start.9
  1249.2 3.1 copy-start.23
  1249.2 11.2 collective-permute-start.10
  1252.2 1.0 copy-start.7
  1253.3 1.0 copy-start.21
  1260.7 3.2 copy-start.5
  1261.8 3.1 copy-start.19
  1261.8 12.7 collective-permute-start.11
  1264.9 1.0 copy-start.3
  1265.9 1.0 copy-start.17
  1275.9 11.6 copy-start.15
  1275.9 17.6 %collective-permute-start.12 = (bf16[2048,128]{1,0:T(8,128)(2,1)S(1)}, bf16[2048,128]{1,0:T(8,128)(2,1)S(1)}, u32[]{:S(2)}, u32[]{:S(2)}) collective-permute-start(bf16[2048,128]{1,0:T(8,128)(2,1)S(1)} %convolution_convert_fusion.1), channel_id=1, source_target_pairs={{0,2},{2,0},{1,3},{3,1},{4,6},{6,4},{5,7},{7,5},{8,10},{10,8},{9,1... | collective-permute-start | bytes 1572872 | tf_op jit(solution)/shard_map/ppermute | solution.py:14
  1288.4 1.0 copy-start.13
  1293.8 1.0 copy-start.11
  1297.2 73.6 %collective-permute-start.13 = (bf16[2048,128]{1,0:T(8,128)(2,1)S(1)}, bf16[2048,128]{1,0:T(8,128)(2,1)S(1)}, u32[]{:S(2)}, u32[]{:S(2)}) collective-permute-start(bf16[2048,128]{1,0:T(8,128)(2,1)S(1)} %convolution_convert_fusion), channel_id=1, source_target_pairs={{0,1},{1,0},{2,3},{3,2},{4,5},{5,4},{6,7},{7,6},{8,9},{9,8},{10,11... | collective-permute-start | bytes 1572872 | tf_op jit(solution)/shard_map/ppermute | solution.py:14
  1357.8 1.4 copy-start.43
  1359.1 0.8 copy-start.40
  1368.2 0.8 copy-start.42
  (12 other events, 9.1 us)
Sparse Core Ops, SparseCore 0:
  1295.9 61.7 all-reduce.4
where the time goes:
time: 1380 us
  blocking collectives  989 us (72%)
  waiting for transfers between devices  228 us (17%)
  starting transfers between devices  93.5 us (7%)
  matrix products  36.7 us (3%)
  local copies, waits for them, and re-layouts  15.7 us (1%)
  between operations  14.6 us (1%)
    psum x1, blocking collectives, rank_total(): return lax.psum(partial_low, 'mp')  498 us
    psum x1, blocking collectives, per_device(): d_low = lax.psum(partial_back, 'mp').astype(jnp.bfloat16)  492 us
    ppermute x14, waiting for transfers between devices, swapped(): return lax.ppermute(block, axis, route)  169 us
    ppermute x14, starting transfers between devices, swapped(): return lax.ppermute(block, axis, route)  93.4 us
    psum x1, waiting for transfers between devices, per_device(): lax.psum(term_d.astype(jnp.bfloat16), 'dp').astype(jnp.float32)  58.6 us
  transfers between devices with their start and end apart: 15, of which 12 were waited for; matrix products, arithmetic and copies ran while one was open for 2% of the time, Pallas kernels for 0%

commit v1 on v0

--- a/solution.py
+++ b/solution.py
@@ -18,9 +18,14 @@
     return jax.vjp(lambda v: jax.nn.gelu(v, approximate=True), pre)[1](cot)[0]
 
 
+def summed(partial):
+    piece = lax.psum_scatter(partial, "mp", scatter_dimension=0, tiled=True)
+    return lax.all_gather(piece.astype(jnp.bfloat16), "mp", axis=0, tiled=True)
+
+
 def rank_total(acts, low_in):
     partial_low = jnp.dot(acts, low_in, preferred_element_type=jnp.float32)
-    return lax.psum(partial_low, "mp")
+    return summed(partial_low)
 
 
 def per_device(acts, diag_weight, cross_weight, low_in, low_out, cotangent):
@@ -47,7 +52,7 @@
     output = jax.nn.gelu(pre, approximate=True).astype(jnp.bfloat16)
     d_pre = gelu_slope(pre, cotangent.astype(jnp.float32)).astype(jnp.bfloat16)
     partial_back = jnp.dot(d_pre, low_out.T, preferred_element_type=jnp.float32)
-    d_low = lax.psum(partial_back, "mp").astype(jnp.bfloat16)
+    d_low = summed(partial_back)
     low_back = jnp.dot(d_low, low_in.T, preferred_element_type=jnp.float32)
     local_in = scale * jnp.dot(acts.T, d_low, preferred_element_type=jnp.float32)
     local_out = scale * jnp.dot(low_b.T, d_pre, preferred_element_type=jnp.float32)

time: 1380 us -> 968 us (0.70)
  blocking collectives: 989 us -> 162 us
  waiting for transfers between devices: 228 us -> 660 us
  starting transfers between devices: 93.5 us -> 72 us
    psum x2 -> x0, blocking collectives: 989 us -> none  [the longest x1 498 us: rank_total(): return lax.psum(partial_low, 'mp')]
    reduce_scatter x0 -> x2, waiting for transfers between devices: none -> 373 us  [summed(): piece = lax.psum_scatter(partial, 'mp', scatter_dimension=0, tiled=True)]
    all_gather x0 -> x2, blocking collectives: none -> 162 us  [summed(): return lax.all_gather(piece.astype(jnp.bfloat16), 'mp', axis=0, tiled=True)]
    ppermute x14, waiting for transfers between devices: 169 us -> 231 us  [swapped(): return lax.ppermute(block, axis, route)]
    ppermute x14, starting transfers between devices: 93.4 us -> 71.9 us  [swapped(): return lax.ppermute(block, axis, route)]
  transfers between devices with their start and end apart: 15 -> 17, of which waited for: 12 -> 14; matrix products, arithmetic and copies ran while one was open for 2% -> 3% of each run, Pallas kernels for 0% -> 0%
where the time goes in v1:
time: 968 us; the launch traced here: 966 us
  waiting for transfers between devices  660 us (68%)
  blocking collectives  162 us (17%)
  starting transfers between devices  72 us (7%)
  matrix products  40.1 us (4%)
  between operations  14.3 us (1%)
  local copies, waits for them, and re-layouts  14 us (1%)
    reduce_scatter x2, waiting for transfers between devices, summed(): piece = lax.psum_scatter(partial, 'mp', scatter_dimension=0, tiled=True)  373 us
    ppermute x14, waiting for transfers between devices, swapped(): return lax.ppermute(block, axis, route)  231 us
    all_gather x2, blocking collectives, summed(): return lax.all_gather(piece.astype(jnp.bfloat16), 'mp', axis=0, tiled=True)  162 us
    ppermute x14, starting transfers between devices, swapped(): return lax.ppermute(block, axis, route)  71.9 us
    psum x1, waiting for transfers between devices, per_device(): lax.psum(term_d.astype(jnp.bfloat16), 'dp').astype(jnp.float32)  55.6 us
  transfers between devices with their start and end apart: 17, of which 14 were waited for; matrix products, arithmetic and copies ran while one was open for 3% of the time, Pallas kernels for 0%

profile of v1, /device:TPU:8, one launch (start us, length us, event | category | flops | bytes accessed | tf_op | source)
XLA Modules:
  0.0 965.8 jit_solution(15311273889378741607)
XLA Ops:
  7.2 2.1 collective-permute-start
  9.3 1.3 fusion.90
  12.2 7.7 collective-permute-start.1
  20.2 11.9 %collective-permute-done.1 = bf16[2048,128]{1,0:T(8,128)(2,1)S(1)} collective-permute-done((bf16[2048,128]{1,0:T(8,128)(2,1)S(1)}, bf16[2048,128]{1,0:T(8,128)(2,1)S(1)}, u32[]{:S(2)}, u32[]{:S(2)}) %collective-permute-start.1) | collective-permute-done | bytes 524320 | tf_op jit(solution)/shard_map/ppermute | solution.py:14
  32.9 1.9 collective-permute-start.2
  35.1 14.7 %collective-permute-done.2 = bf16[2048,128]{1,0:T(8,128)(2,1)S(1)} collective-permute-done((bf16[2048,128]{1,0:T(8,128)(2,1)S(1)}, bf16[2048,128]{1,0:T(8,128)(2,1)S(1)}, u32[]{:S(2)}, u32[]{:S(2)}) %collective-permute-start.2) | collective-permute-done | bytes 524320 | tf_op jit(solution)/shard_map/ppermute | solution.py:14
  50.6 1.9 collective-permute-start.3
  52.8 12.2 %collective-permute-done.3 = bf16[2048,128]{1,0:T(8,128)(2,1)S(1)} collective-permute-done((bf16[2048,128]{1,0:T(8,128)(2,1)S(1)}, bf16[2048,128]{1,0:T(8,128)(2,1)S(1)}, u32[]{:S(2)}, u32[]{:S(2)}) %collective-permute-start.3) | collective-permute-done | bytes 524320 | tf_op jit(solution)/shard_map/ppermute | solution.py:14
  65.8 1.9 collective-permute-start.4
  68.0 23.4 %collective-permute-done.4 = bf16[2048,128]{1,0:T(8,128)(2,1)S(1)} collective-permute-done((bf16[2048,128]{1,0:T(8,128)(2,1)S(1)}, bf16[2048,128]{1,0:T(8,128)(2,1)S(1)}, u32[]{:S(2)}, u32[]{:S(2)}) %collective-permute-start.4) | collective-permute-done | bytes 524320 | tf_op jit(solution)/shard_map/ppermute | solution.py:14
  92.2 5.0 collective-permute-start.5
  97.3 1.3 fusion.120
  98.9 44.4 %collective-permute-done.5 = bf16[2048,128]{1,0:T(8,128)(2,1)} collective-permute-done((bf16[2048,128]{1,0:T(8,128)(2,1)S(1)}, bf16[2048,128]{1,0:T(8,128)(2,1)}, u32[]{:S(2)}, u32[]{:S(2)}) %collective-permute-start.5) | collective-permute-done | bytes 524320 | tf_op jit(solution)/shard_map/ppermute | solution.py:14
  143.3 1.3 fusion.6
  144.6 22.4 %collective-permute-start.6 = (bf16[2048,128]{1,0:T(8,128)(2,1)S(1)}, bf16[2048,128]{1,0:T(8,128)(2,1)}, u32[]{:S(2)}, u32[]{:S(2)}) collective-permute-start(bf16[2048,128]{1,0:T(8,128)(2,1)S(1)} %fusion.6), channel_id=1, source_target_pairs={{0,64},{64,0},{1,65},{65,1},{2,66},{66,2},{3,67},{67,3},{4,68},{68... | collective-permute-start | bytes 1572872 | tf_op jit(solution)/shard_map/ppermute | solution.py:14
  167.1 190.0 %reduce-scatter.3.cloned.1.call-done = f32[16,64]{1,0:T(8,128)} async-done(((f32[2048,64]{1,0:T(8,128)}), f32[16,64]{1,0:T(8,128)}) %reduce-scatter.3.cloned.1.call-update) | async-done | bytes 4112 | tf_op jit(solution)/shard_map/reduce_scatter | solution.py:22
  357.8 81.0 %all_gather.6 = bf16[2048,64]{1,0:T(8,128)(2,1)S(1)} all-gather(bf16[16,64]{1,0:T(8,128)(2,1)S(1)} %convert_element_type.179), channel_id=1, replica_groups=mesh['dp'=4,'mp'=128] {'mp'}, dimensions={0}, use_global_device_ids=true | all-gather | bytes 264192 | tf_op jit(solution)/shard_map/all_gather | solution.py:23
  439.1 1.4 convolution_add_fusion.7
  440.5 1.8 fusion.46
  442.6 10.4 %collective-permute-start.7 = (bf16[2048,128]{1,0:T(8,128)(2,1)S(1)}, bf16[2048,128]{1,0:T(8,128)(2,1)S(1)}, u32[]{:S(2)}, u32[]{:S(2)}) collective-permute-start(bf16[2048,128]{1,0:T(8,128)(2,1)S(1)} %convolution_convert_fusion.6), channel_id=1, source_target_pairs={{0,64},{64,0},{1,65},{65,1},{2,66},{66,2},{3,67},{67,3},{4,68},{68... | collective-permute-start | bytes 1572872 | tf_op jit(solution)/shard_map/ppermute | solution.py:14
  453.1 44.2 %collective-permute-done.7 = bf16[2048,128]{1,0:T(8,128)(2,1)S(1)} collective-permute-done((bf16[2048,128]{1,0:T(8,128)(2,1)S(1)}, bf16[2048,128]{1,0:T(8,128)(2,1)S(1)}, u32[]{:S(2)}, u32[]{:S(2)}) %collective-permute-start.7) | collective-permute-done | bytes 524320 | tf_op jit(solution)/shard_map/ppermute | solution.py:14
  497.9 4.7 collective-permute-start.8
  502.6 1.3 fusion.121
  503.9 43.8 %collective-permute-done.8 = bf16[2048,128]{1,0:T(8,128)(2,1)} collective-permute-done((bf16[2048,128]{1,0:T(8,128)(2,1)S(1)}, bf16[2048,128]{1,0:T(8,128)(2,1)}, u32[]{:S(2)}, u32[]{:S(2)}) %collective-permute-start.8) | collective-permute-done | bytes 524320 | tf_op jit(solution)/shard_map/ppermute | solution.py:14
  547.7 1.4 fusion.7
  549.4 1.9 collective-permute-start.9
  552.3 2.0 fusion.27
  555.3 18.4 %collective-permute-done.9 = bf16[2048,128]{1,0:T(8,128)(2,1)S(1)} collective-permute-done((bf16[2048,128]{1,0:T(8,128)(2,1)S(1)}, bf16[2048,128]{1,0:T(8,128)(2,1)S(1)}, u32[]{:S(2)}, u32[]{:S(2)}) %collective-permute-start.9) | collective-permute-done | bytes 524320 | tf_op jit(solution)/shard_map/ppermute | solution.py:14
  573.7 1.1 fusion.8
  574.7 1.1 convolution_convert_fusion.3
  575.8 1.9 collective-permute-start.10
  578.7 2.0 fusion.28
  580.7 183.4 %reduce-scatter.5.cloned.1.call-done = f32[16,64]{1,0:T(8,128)} async-done(((f32[2048,64]{1,0:T(8,128)}), f32[16,64]{1,0:T(8,128)}) %reduce-scatter.5.cloned.1.call-update) | async-done | bytes 4112 | tf_op jit(solution)/shard_map/reduce_scatter | solution.py:22
  764.8 81.2 %all_gather.7 = bf16[2048,64]{1,0:T(8,128)(2,1)S(1)} all-gather(bf16[16,64]{1,0:T(8,128)(2,1)S(1)} %convert_element_type.203), channel_id=1, replica_groups=mesh['dp'=4,'mp'=128] {'mp'}, dimensions={0}, use_global_device_ids=true | all-gather | bytes 264192 | tf_op jit(solution)/shard_map/all_gather | solution.py:23
  846.9 1.4 fusion.9
  848.6 4.1 collective-permute-start.11
  852.7 1.0 fusion.36
  853.7 1.0 fusion.29
  854.7 1.0 fusion.37
  856.8 9.5 collective-permute-done.11
  866.3 1.1 fusion.10
  867.7 3.9 collective-permute-start.12
  875.5 7.7 collective-permute-done.12
  883.2 1.1 fusion.11
  886.8 1.9 collective-permute-start.13
  888.8 55.6 %all-reduce.3.cloned.1.call-done = (bf16[1,128,128]{1,2,0:T(8,128)(2,1)}, bf16[1,128,128]{1,2,0:T(8,128)(2,1)}, bf16[1,128,128]{1,2,0:T(8,128)(2,1)}, bf16[1,128...) async-done(((bf16[1,128,128]{1,2,0:T(8,128)(2,1)}, ...) | async-done | bytes 491536 | tf_op jit(solution)/shard_map/psum | solution.py:71
  944.3 1.3 convert_element_type.223
  957.4 1.9 fusion.12
  (140 shorter events, 32.7 us)
Async XLA Ops:
  7.2 433.3 %copy-start = (bf16[64,128]{1,0:T(8,128)(2,1)S(1)}, bf16[64,128]{1,0:T(8,128)(2,1)}, u32[]{:S(2)}) copy-start(bf16[64,128]{1,0:T(8,128)(2,1)} %param.10) | copy-start | bytes 49156
  7.2 4.2 copy-start.22
  7.2 349.9 %reduce-scatter.3.cloned.1.call-start = ((), (), s32[]{:S(2)}) async-start(), calls=%async_computation.2 | async-start | bytes 1056768 | tf_op jit(solution)/shard_map/reduce_scatter | solution.py:22
  7.2 4.1 collective-permute-start
  10.6 9.3 copy-start.23
  11.4 0.8 copy-start.12
  12.2 19.9 %collective-permute-start.1 = (bf16[2048,128]{1,0:T(8,128)(2,1)S(1)}, bf16[2048,128]{1,0:T(8,128)(2,1)S(1)}, u32[]{:S(2)}, u32[]{:S(2)}) collective-permute-start(bf16[2048,128]{1,0:T(8,128)(2,1)S(1)} %fusion.1), channel_id=1, source_target_pairs={{0,2},{2,0},{1,3},{3,1},{4,6},{6,4},{5,7},{7,5},{8,10},{10,8},{9,1... | collective-permute-start | bytes 1572872 | tf_op jit(solution)/shard_map/ppermute | solution.py:14
  32.1 0.8 copy-start.14
  32.9 16.8 %collective-permute-start.2 = (bf16[2048,128]{1,0:T(8,128)(2,1)S(1)}, bf16[2048,128]{1,0:T(8,128)(2,1)S(1)}, u32[]{:S(2)}, u32[]{:S(2)}) collective-permute-start(bf16[2048,128]{1,0:T(8,128)(2,1)S(1)} %fusion.2), channel_id=1, source_target_pairs={{0,4},{4,0},{1,5},{5,1},{2,6},{6,2},{3,7},{7,3},{8,12},{12,8},{9,1... | collective-permute-start | bytes 1572872 | tf_op jit(solution)/shard_map/ppermute | solution.py:14
  49.8 0.8 copy-start.16
  50.6 2.2 copy-start.2
  50.6 14.4 %collective-permute-start.3 = (bf16[2048,128]{1,0:T(8,128)(2,1)S(1)}, bf16[2048,128]{1,0:T(8,128)(2,1)S(1)}, u32[]{:S(2)}, u32[]{:S(2)}) collective-permute-start(bf16[2048,128]{1,0:T(8,128)(2,1)S(1)} %fusion.3), channel_id=1, source_target_pairs={{0,8},{8,0},{1,9},{9,1},{2,10},{10,2},{3,11},{11,3},{4,12},{12,4},... | collective-permute-start | bytes 1572872 | tf_op jit(solution)/shard_map/ppermute | solution.py:14
  65.0 0.8 copy-start.18
  65.8 2.2 copy-start.4
  65.8 25.6 %collective-permute-start.4 = (bf16[2048,128]{1,0:T(8,128)(2,1)S(1)}, bf16[2048,128]{1,0:T(8,128)(2,1)S(1)}, u32[]{:S(2)}, u32[]{:S(2)}) collective-permute-start(bf16[2048,128]{1,0:T(8,128)(2,1)S(1)} %fusion.4), channel_id=1, source_target_pairs={{0,16},{16,0},{1,17},{17,1},{2,18},{18,2},{3,19},{19,3},{4,20},{20... | collective-permute-start | bytes 1572872 | tf_op jit(solution)/shard_map/ppermute | solution.py:14
  68.0 29.3 %copy-start.1 = (bf16[2048,128]{1,0:T(8,128)(2,1)S(1)}, bf16[2048,128]{1,0:T(8,128)(2,1)}, u32[]{:S(2)}) copy-start(bf16[2048,128]{1,0:T(8,128)(2,1)} %param.6) | copy-start | bytes 1572868
  68.0 29.3 %copy-start.24 = (bf16[128,64]{0,1:T(8,128)(2,1)S(1)}, bf16[128,64]{0,1:T(8,128)(2,1)}, u32[]{:S(2)}) copy-start(bf16[128,64]{0,1:T(8,128)(2,1)} %param.9) | copy-start | bytes 49156
  91.4 0.8 copy-start.20
  92.2 6.4 copy-start.6
  92.2 51.1 %collective-permute-start.5 = (bf16[2048,128]{1,0:T(8,128)(2,1)S(1)}, bf16[2048,128]{1,0:T(8,128)(2,1)}, u32[]{:S(2)}, u32[]{:S(2)}) collective-permute-start(bf16[2048,128]{1,0:T(8,128)(2,1)S(1)} %fusion.5), channel_id=1, source_target_pairs={{0,32},{32,0},{1,33},{33,1},{2,34},{34,2},{3,35},{35,3},{4,36},{36... | collective-permute-start | bytes 1572872 | tf_op jit(solution)/shard_map/ppermute | solution.py:14
  98.6 665.5 %reduce-scatter.5.cloned.1.call-start = ((), (), s32[]{:S(2)}) async-start(), calls=%async_computation.3 | async-start | bytes 1056768 | tf_op jit(solution)/shard_map/reduce_scatter | solution.py:22
  144.6 294.4 %copy-start.8 = (bf16[2048,128]{1,0:T(8,128)(2,1)}, bf16[2048,128]{1,0:T(8,128)(2,1)S(1)}, u32[]{:S(2)}) copy-start(bf16[2048,128]{1,0:T(8,128)(2,1)S(1)} %fusion.6) | copy-start | bytes 1572868
  144.6 294.4 %collective-permute-start.6 = (bf16[2048,128]{1,0:T(8,128)(2,1)S(1)}, bf16[2048,128]{1,0:T(8,128)(2,1)}, u32[]{:S(2)}, u32[]{:S(2)}) collective-permute-start(bf16[2048,128]{1,0:T(8,128)(2,1)S(1)} %fusion.6), channel_id=1, source_target_pairs={{0,64},{64,0},{1,65},{65,1},{2,66},{66,2},{3,67},{67,3},{4,68},{68... | collective-permute-start | bytes 1572872 | tf_op jit(solution)/shard_map/ppermute | solution.py:14
  438.8 1.7 copy-start.10
  439.1 1.4 copy-start.40
  442.6 54.6 %collective-permute-start.7 = (bf16[2048,128]{1,0:T(8,128)(2,1)S(1)}, bf16[2048,128]{1,0:T(8,128)(2,1)S(1)}, u32[]{:S(2)}, u32[]{:S(2)}) collective-permute-start(bf16[2048,128]{1,0:T(8,128)(2,1)S(1)} %convolution_convert_fusion.6), channel_id=1, source_target_pairs={{0,64},{64,0},{1,65},{65,1},{2,66},{66,2},{3,67},{67,3},{4,68},{68... | collective-permute-start | bytes 1572872 | tf_op jit(solution)/shard_map/ppermute | solution.py:14
  497.9 49.9 %collective-permute-start.8 = (bf16[2048,128]{1,0:T(8,128)(2,1)S(1)}, bf16[2048,128]{1,0:T(8,128)(2,1)}, u32[]{:S(2)}, u32[]{:S(2)}) collective-permute-start(bf16[2048,128]{1,0:T(8,128)(2,1)S(1)} %convolution_convert_fusion.5), channel_id=1, source_target_pairs={{0,32},{32,0},{1,33},{33,1},{2,34},{34,2},{3,35},{35,3},{4,36},{36... | collective-permute-start | bytes 1572872 | tf_op jit(solution)/shard_map/ppermute | solution.py:14
  503.9 440.4 %all-reduce.3.cloned.1.call-start = ((), (), s32[]{:S(2)}) async-start(), calls=%async_computation.4 | async-start | bytes 983040 | tf_op jit(solution)/shard_map/psum | solution.py:71
  549.1 2.2 copy-start.9
  549.4 24.2 %collective-permute-start.9 = (bf16[2048,128]{1,0:T(8,128)(2,1)S(1)}, bf16[2048,128]{1,0:T(8,128)(2,1)S(1)}, u32[]{:S(2)}, u32[]{:S(2)}) collective-permute-start(bf16[2048,128]{1,0:T(8,128)(2,1)S(1)} %convolution_convert_fusion.4), channel_id=1, source_target_pairs={{0,16},{16,0},{1,17},{17,1},{2,18},{18,2},{3,19},{19,3},{4,20},{20... | collective-permute-start | bytes 1572872 | tf_op jit(solution)/shard_map/ppermute | solution.py:14
  552.3 2.1 copy-start.11
  574.7 3.0 copy-start.7
  575.8 271.1 %collective-permute-start.10 = (bf16[2048,128]{1,0:T(8,128)(2,1)}, bf16[2048,128]{1,0:T(8,128)(2,1)}, u32[]{:S(2)}, u32[]{:S(2)}) collective-permute-start(bf16[2048,128]{1,0:T(8,128)(2,1)} %convolution_convert_fusion.3), channel_id=1, source_target_pairs={{0,8},{8,0},{1,9},{9,1},{2,10},{10,2},{3,11},{11,3},{4,12},{12,4},... | collective-permute-start | bytes 1572872 | tf_op jit(solution)/shard_map/ppermute | solution.py:14
  848.3 4.5 copy-start.5
  848.6 5.1 copy-start.21
  848.6 17.7 %collective-permute-start.11 = (bf16[2048,128]{1,0:T(8,128)(2,1)S(1)}, bf16[2048,128]{1,0:T(8,128)(2,1)S(1)}, u32[]{:S(2)}, u32[]{:S(2)}) collective-permute-start(bf16[2048,128]{1,0:T(8,128)(2,1)S(1)} %convolution_convert_fusion.2), channel_id=1, source_target_pairs={{0,4},{4,0},{1,5},{5,1},{2,6},{6,2},{3,7},{7,3},{8,12},{12,8},{9,1... | collective-permute-start | bytes 1572872 | tf_op jit(solution)/shard_map/ppermute | solution.py:14
  853.7 1.0 copy-start.3
  854.7 1.0 copy-start.19
  867.7 4.9 copy-start.17
  867.7 15.5 %collective-permute-start.12 = (bf16[2048,128]{1,0:T(8,128)(2,1)S(1)}, bf16[2048,128]{1,0:T(8,128)(2,1)S(1)}, u32[]{:S(2)}, u32[]{:S(2)}) collective-permute-start(bf16[2048,128]{1,0:T(8,128)(2,1)S(1)} %convolution_convert_fusion.1), channel_id=1, source_target_pairs={{0,2},{2,0},{1,3},{3,1},{4,6},{6,4},{5,7},{7,5},{8,10},{10,8},{9,1... | collective-permute-start | bytes 1572872 | tf_op jit(solution)/shard_map/ppermute | solution.py:14
  873.5 1.0 copy-start.15
  884.3 1.0 copy-start.13
  886.8 70.6 %collective-permute-start.13 = (bf16[2048,128]{1,0:T(8,128)(2,1)S(1)}, bf16[2048,128]{1,0:T(8,128)(2,1)S(1)}, u32[]{:S(2)}, u32[]{:S(2)}) collective-permute-start(bf16[2048,128]{1,0:T(8,128)(2,1)S(1)} %convolution_convert_fusion), channel_id=1, source_target_pairs={{0,1},{1,0},{2,3},{3,2},{4,5},{5,4},{6,7},{7,6},{8,9},{9,8},{10,11... | collective-permute-start | bytes 1572872 | tf_op jit(solution)/shard_map/ppermute | solution.py:14
  944.3 1.4 copy-start.39
  946.4 0.8 copy-start.35
  947.2 0.8 copy-start.34
  948.0 0.8 copy-start.33
  954.8 0.8 copy-start.38
  (10 other events, 7.6 us)
Sparse Core Ops, SparseCore 0:
  98.7 258.3 reduce-scatter.2
  504.0 260.0 reduce-scatter.4
  886.4 57.8 all-reduce.2

commit v2 on v0

v2 whole, which is shorter than its diff:
```python
import functools

import jax
import jax.numpy as jnp
from jax import lax
from jax.experimental import pallas as pl
from jax.experimental.pallas import tpu as pltpu
from jax.sharding import PartitionSpec as P

MESH = pl.DeviceIdType.MESH
BF = jnp.bfloat16
F32 = jnp.float32
BLK = 128
RANK = 64
ROWS = 8
NEAR = 3
FAR = 4
PIECE = 2 * BLK + RANK // FAR


def flipped(index, stride):
    return index + stride - 2 * stride * ((index // stride) % 2)


def mm(a, b):
    return lax.dot_general(a, b, (((1,), (0,)), ((), ())), preferred_element_type=F32)


def mm_nt(a, b):
    return lax.dot_general(a, b, (((1,), (1,)), ((), ())), preferred_element_type=F32)


def mm_tn(a, b):
    return lax.dot_general(a, b, (((0,), (0,)), ((), ())), preferred_element_type=F32)


def kernel(
    nx, nz, scale,
    acts, cot, diag, cross, packed_w, lin2,
    out, gacts, gdiag, gcross, glin, glout,
    near_in, near_z, far, cot_far, out_snd, out_rcv, d_snd, d_rcv,
    weights, upper, grad_snd, grad_rcv, red, rs_snd, rs_rcv, fin_snd, fin_rcv,
    near_dz, q_snd, q_rcv, sg_snd, sg_rcv, gl_snd, gl_rcv,
    lp_snd, lp_rcv, lb_snd, lb_rcv, low_u, dacc, db_snd, db_rcv, dl_snd, dl_all,
    f_send, f_recv, b_send, b_recv, w_send, w_recv, x_send, x_recv,
    a_send, a_recv, low_send, low_recv, g_send, g_recv, rs_send, rs_recv, s_send, s_recv,
):
    x = lax.axis_index("dp")
    n = lax.axis_index("mp")
    z, r = n // ROWS, n % ROWS

    def at_z(zz):
        return (x, zz * ROWS + r)

    def at_r(rr):
        return (x, z * ROWS + rr)

    def at_x(xx):
        return (xx, n)

    def send(src, dst, ssem, rsem, where):
        pltpu.make_async_remote_copy(
            src_ref=src, dst_ref=dst, send_sem=ssem, recv_sem=rsem,
            device_id=where, device_id_type=MESH,
        ).start()

    def take(ref, sem):
        pltpu.make_async_copy(ref, ref, sem).wait()

    barrier = pltpu.get_barrier_semaphore()

    def greet(count, where):
        def one(k, _):
            pl.semaphore_signal(barrier, inc=1, device_id=where(k), device_id_type=MESH)
            return 0
        lax.fori_loop(1, count, one, 0)

    greet(nz, lambda k: at_z((z + k) % nz))
    greet(ROWS, lambda k: at_r((r + k) % ROWS))
    greet(nx, lambda k: at_x((x + k) % nx))
    pl.semaphore_wait(barrier, nz + ROWS + nx - 3)

    hz = nz // 2
    half = hz * RANK

    def chunk(ref, j):
        return ref.at[j // 2, pl.ds((j % 2) * hz, hz)]

    def load(ref, j):
        return ref[j // 2, pl.ds((j % 2) * hz, hz)].reshape(half, BLK)

    def near_send(src, dst, j, section, ssem, rsem):
        send(chunk(src, j), chunk(dst, j), ssem, rsem, (x, flipped(n, 1 << section)))

    for j in range(4):
        near_send(acts, near_in.at[0], j, 0, f_send.at[0], f_recv.at[0, j])

    steps_up = nz // 2
    steps_down = nz - 1 - steps_up

    def w_pass(k):
        up, down = (z + nz - k) % nz, (z + k) % nz

        def hop(piece, where, direction):
            src = packed_w.at[x] if k == 0 else weights.at[x, piece]
            send(src, weights.at[x, piece], w_send.at[direction], w_recv.at[piece], at_z(where))

        if k < steps_up:
            hop(up, (z + 1) % nz, 0)
        if k < steps_down:
            hop(down, (z + nz - 1) % nz, 1)

    def w_take(k):
        def one(piece):
            take(weights.at[x, piece], w_recv.at[piece])
            def other(d, _):
                send(weights.at[x, piece], weights.at[x, piece], x_send.at[0], x_recv.at[x, piece], at_x((x + d) % nx))
                return 0
            lax.fori_loop(1, nx, other, 0)
        if k <= steps_up:
            one((z + nz - k) % nz)
        if k <= steps_down:
            one((z + k) % nz)

    w_pass(0)
    for q in range(FAR):
        weights[q, z] = packed_w[q]

    for j in range(2):
        zs = pl.ds(j * hz, hz)
        part = mm(acts[0, zs].reshape(half, BLK), lin2[0]) + mm(acts[1, zs].reshape(half, BLK), lin2[1])
        lp_snd[zs] = part.reshape(hz, RANK, BLK).astype(BF)

    def far_all(count, fn):
        def one(k, _):
            fn((z + k) % count)
            return 0
        lax.fori_loop(1, count, one, 0)

    far_all(nz, lambda zz: send(lp_snd.at[zz], lp_rcv.at[z], low_send.at[0], low_recv.at[0], at_z(zz)))
    lp_rcv[z] = lp_snd[z]

    def near_forward(section, src, dst, after):
        both = jnp.concatenate([diag[section], cross[section]], axis=0)
        for j in range(4):
            take(chunk(near_in.at[section], j), f_recv.at[section, j])
            fresh = mm(jnp.concatenate([load(src, j), load(near_in.at[section], j)], axis=1), both)
            dst[j // 2, pl.ds((j % 2) * hz, hz)] = fresh.astype(BF).reshape(hz, RANK, BLK)
            after(j)

    def after0(j):
        near_send(near_z.at[0], near_in.at[1], j, 1, f_send.at[1], f_recv.at[1, j])

    near_forward(0, acts, near_z.at[0], after0)

    far_all(nz, lambda zz: send(cot.at[:, zz], cot_far.at[z], a_send.at[0], a_recv.at[0], at_z(zz)))
    cot_far[z] = cot[:, z]

    def ring(k):
        if k <= steps_up:
            w_take(k)
            w_pass(k)

    def after1(j):
        near_send(near_z.at[1], near_in.at[2], j, 2, f_send.at[2], f_recv.at[2, j])
        ring(1 + j)

    near_forward(1, near_z.at[0], near_z.at[1], after1)

    take(lp_rcv.at[pl.ds(0, nz - 1)], low_recv.at[0])
    total = lp_rcv[0].astype(F32)
    for zz in range(1, nz):
        total = total + lp_rcv[zz].astype(F32)
    lb_snd[...] = total

    def plane_all(src, dst, sem):
        def one(k, _):
            send(src, dst.at[r], low_send.at[sem], low_recv.at[sem], at_r((r + k) % ROWS))
            return 0
        lax.fori_loop(1, ROWS, one, 0)

    plane_all(lb_snd, lb_rcv, 1)
    lb_rcv[r] = lb_snd[...]

    def after2(j):
        if j % 2:
            c = j // 2
            far_all(nz, lambda zz: send(near_z.at[2, c, zz], far.at[0, z, c], a_send.at[1], a_recv.at[1], at_z(zz)))
            far[0, z, c] = near_z[2, c, z]
        ring(5 + j)

    near_forward(2, near_z.at[1], near_z.at[2], after2)
    for k in range(9, steps_up + 1):
        ring(k)

    take(lb_rcv.at[pl.ds(0, ROWS - 1)], low_recv.at[1])
    total = lb_rcv[0]
    for rr in range(1, ROWS):
        total = total + lb_rcv[rr]
    low_u[0:RANK] = total[:, :RANK].astype(BF)
    low_u[RANK:BLK] = total[:, RANK:].astype(BF)

    take(far.at[0, pl.ds(0, nz - 1)], a_recv.at[1])

    def weights_ready(q):
        @pl.when(x != q)
        def _():
            def one(k, _):
                piece = (z + k) % nz
                take(weights.at[q, piece], x_recv.at[q, piece])
                return 0
            lax.fori_loop(1, nz, one, 0)

    def tile(ref, b):
        return ref[b].reshape(BLK, BLK)

    def pair(ref, b, stride):
        return jnp.concatenate([tile(ref, b), tile(ref, flipped(b, stride))], axis=1)

    for q in range(FAR - 1):
        weights_ready(q)

        def forward(b, _, q=q):
            fresh = mm(pair(far.at[q], b, 1 << q), weights[q, b, 0:2 * BLK])
            far[q + 1, b] = fresh.astype(BF).reshape(2, RANK, BLK)
            return 0
        lax.fori_loop(0, nz, forward, 0, unroll=2)

    weights_ready(FAR - 1)
    take(cot_far.at[pl.ds(0, nz - 1)], a_recv.at[0])
    dacc[...] = jnp.zeros_like(dacc)
    root = 0.7978845608028654

    def last(k, _):
        b = (z + k) % nz
        lout = jnp.concatenate([weights[q, b, 2 * BLK:PIECE] for q in range(FAR)], axis=0)
        pre = mm(pair(far.at[FAR - 1], b, 1 << (FAR - 1)), weights[FAR - 1, b, 0:2 * BLK])
        pre = pre + mm(low_u[...], lout)
        square = pre * pre
        th = jnp.tanh(root * (pre * (1.0 + 0.044715 * square)))
        side = 0.5 * (1.0 + th)
        out_snd[b] = (pre * side).astype(BF).reshape(2, RANK, BLK)
        slope = side + 0.5 * pre * (1.0 - th * th) * (root * (1.0 + 3 * 0.044715 * square))
        dpre = (cot_far[b].reshape(BLK, BLK).astype(F32) * slope).astype(BF)
        upper[FAR, b] = dpre.reshape(2, RANK, BLK)
        dacc[...] += mm_nt(dpre, lout)

        @pl.when(b != z)
        def _():
            send(out_snd.at[b], out_rcv.at[:, z], a_send.at[2], a_recv.at[2], at_z(b))
        return 0

    lax.fori_loop(1, nz + 1, last, 0)
    out_rcv[:, z] = out_snd[z]
    db_snd[...] = jnp.concatenate([dacc[0:RANK], dacc[RANK:BLK]], axis=1)
    plane_all(db_snd, db_rcv, 2)
    db_rcv[r] = db_snd[...]

    for q in range(FAR - 1, -1, -1):
        def backward(k, _, q=q):
            b = (z + k) % nz
            o = flipped(b, 1 << q)
            here = tile(upper.at[q + 1], b)
            grad_snd[q, b, 0:2 * BLK] = mm_tn(pair(far.at[q], b, 1 << q), here).astype(BF)
            if q == FAR - 1:
                gl = mm_tn(low_u[...], here).astype(BF)
                for p in range(FAR):
                    grad_snd[p, b, 2 * BLK:PIECE] = gl[p * (RANK // FAR):(p + 1) * (RANK // FAR)]
            both = jnp.concatenate([weights[q, b, 0:BLK], weights[q, o, BLK:2 * BLK]], axis=1)
            back = mm_nt(jnp.concatenate([here, tile(upper.at[q + 1], o)], axis=1), both)
            upper[q, b] = back.astype(BF).reshape(2, RANK, BLK)
            if q == 0:
                @pl.when(b != z)
                def _():
                    send(upper.at[0, b], d_rcv.at[:, z], a_send.at[3], a_recv.at[3], at_z(b))
            return 0
        lax.fori_loop(1, nz + 1, backward, 0, unroll=2 if q else 1)

        @pl.when(x != q)
        def _():
            send(grad_snd.at[q], grad_rcv.at[x], g_send.at[0], g_recv.at[x], (q, n))

        if q == FAR - 1:
            take(db_rcv.at[pl.ds(0, ROWS - 1)], low_recv.at[2])
            total = db_rcv[0]
            for rr in range(1, ROWS):
                total = total + db_rcv[rr]
            dl_snd[...] = total.astype(BF)
            far_all(nz, lambda zz: send(dl_snd, dl_all.at[z], low_send.at[3], low_recv.at[3], at_z(zz)))
            dl_all[z] = dl_snd[...]
    d_rcv[:, z] = upper[0, z]

    def red_all():
        for d in range(1, nx):
            take(grad_rcv.at[(x + d) % nx], g_recv.at[(x + d) % nx])

        def one(b, _):
            total = grad_snd[x, b].astype(F32)
            for d in range(1, nx):
                total = total + grad_rcv[(x + d) % nx, b].astype(F32)
            red[b] = total.astype(BF)
            return 0
        lax.fori_loop(0, nz, one, 0)

    def rs_step(k):
        up, down = (z + steps_up + 1 - k) % nz, (z + nz - (steps_down + 1 - k)) % nz
        for direction, target, where, count in ((0, up, (z + 1) % nz, steps_up), (1, down, (z + nz - 1) % nz, steps_down)):
            if k > count:
                continue
            if k == 1:
                src = red.at[target]
            else:
                take(rs_rcv.at[direction, k - 2], rs_recv.at[direction, k - 2])
                rs_snd[direction, k - 1] = (rs_rcv[direction, k - 2].astype(F32) + red[target].astype(F32)).astype(BF)
                src = rs_snd.at[direction, k - 1]
            send(src, rs_rcv.at[direction, k - 1], rs_send.at[direction], rs_recv.at[direction, k - 1], at_z(where))

    take(d_rcv.at[:, pl.ds(0, nz - 1)], a_recv.at[3])

    def near_q(section, src, j):
        q_snd[section, j // 2, pl.ds((j % 2) * hz, hz)] = mm_nt(load(src, j), cross[section]).astype(BF).reshape(hz, RANK, BLK)
        near_send(q_snd.at[section], q_rcv.at[section], j, section, b_send.at[section], b_recv.at[section, j])

    def near_grad(section, state, dz):
        total = None
        for j in range(4):
            lhs = jnp.concatenate([load(state, j), load(near_in.at[section], j)], axis=1)
            part = mm_tn(lhs, load(dz, j))
            total = part if total is None else total + part
        sg_snd[section] = total.astype(BF)
        def other(d, _):
            send(sg_snd.at[section], sg_rcv.at[x, section], s_send.at[0], s_recv.at[section, x], at_x((x + d) % nx))
            return 0
        lax.fori_loop(1, nx, other, 0)
        sg_rcv[x, section] = sg_snd[section]

    for j in range(4):
        near_q(2, d_rcv, j)
    near_grad(2, near_z.at[1], d_rcv)
    red_all()
    rs_step(1)

    def near_back(section, src, j):
        take(chunk(q_rcv.at[section], j), b_recv.at[section, j])
        return mm_nt(load(src, j), diag[section]) + load(q_rcv.at[section], j).astype(F32)

    for section, src, state in ((2, d_rcv, None), (1, near_dz.at[1], near_z.at[0])):
        dst = near_dz.at[section - 1]
        for j in range(4):
            back = near_back(section, src, j)
            dst[j // 2, pl.ds((j % 2) * hz, hz)] = back.astype(BF).reshape(hz, RANK, BLK)
            near_q(section - 1, dst, j)
        if section == 2:
            near_grad(1, near_z.at[0], near_dz.at[1])
        else:
            near_grad(0, acts, near_dz.at[0])
        for k in range(2 + 3 * (2 - section), 5 + 3 * (2 - section)):
            if k <= steps_up:
                rs_step(k)

    take(dl_all.at[pl.ds(0, nz - 1)], low_recv.at[3])
    total = None
    for j in range(2):
        zs = pl.ds(j * hz, hz)
        dl = dl_all[zs].reshape(half, BLK)
        part = (mm_tn(dl, acts[0, zs].reshape(half, BLK))[0:RANK]
                + mm_tn(dl, acts[1, zs].reshape(half, BLK))[RANK:BLK])
        total = part if total is None else total + part
    gl_snd[...] = total.astype(BF)
    def other(d, _):
        send(gl_snd, gl_rcv.at[x], s_send.at[1], s_recv.at[NEAR, x], at_x((x + d) % nx))
        return 0
    lax.fori_loop(1, nx, other, 0)
    gl_rcv[x] = gl_snd[...]

    for k in range(8, steps_up + 1):
        rs_step(k)

    for j in range(4):
        zs = pl.ds((j % 2) * hz, hz)
        back = near_back(0, near_dz.at[0], j) + mm_nt(dl_all[zs].reshape(half, BLK), lin2[j // 2])
        gacts[j // 2, zs] = back.astype(BF).reshape(hz, RANK, BLK)

    take(rs_rcv.at[0, steps_up - 1], rs_recv.at[0, steps_up - 1])
    total = red[z].astype(F32) + rs_rcv[0, steps_up - 1].astype(F32)
    if steps_down:
        take(rs_rcv.at[1, steps_down - 1], rs_recv.at[1, steps_down - 1])
        total = total + rs_rcv[1, steps_down - 1].astype(F32)
    fin_snd[...] = total.astype(BF)
    def final(d, _):
        send(fin_snd, fin_rcv.at[x], g_send.at[1], g_recv.at[nx + x], at_x((x + d) % nx))
        return 0
    lax.fori_loop(1, nx, final, 0)
    fin_rcv[x] = fin_snd[...]

    take(out_rcv.at[:, pl.ds(0, nz - 1)], a_recv.at[2])
    out[...] = out_rcv[...]

    for section in range(NEAR):
        for d in range(1, nx):
            take(sg_rcv.at[(x + d) % nx, section], s_recv.at[section, (x + d) % nx])
        total = sg_rcv[0, section].astype(F32)
        for xx in range(1, nx):
            total = total + sg_rcv[xx, section].astype(F32)
        total = total * scale
        gdiag[section] = total[0:BLK]
        gcross[section] = total[BLK:2 * BLK]
    for d in range(1, nx):
        take(gl_rcv.at[(x + d) % nx], s_recv.at[NEAR, (x + d) % nx])
    total = gl_rcv[0].astype(F32)
    for xx in range(1, nx):
        total = total + gl_rcv[xx].astype(F32)
    glin[...] = total * scale
    for d in range(1, nx):
        take(fin_rcv.at[(x + d) % nx], g_recv.at[nx + (x + d) % nx])
    for q in range(FAR):
        total = fin_rcv[q].astype(F32) * scale
        gdiag[NEAR + q] = total[0:BLK]
        gcross[NEAR + q] = total[BLK:2 * BLK]
        glout[q] = total[2 * BLK:PIECE]

    for section in range(NEAR):
        take(near_in.at[section], f_send.at[section])
        take(q_snd.at[section], b_send.at[section])
    take(weights.at[0, pl.ds(0, steps_up)], w_send.at[0])
    if steps_down:
        take(weights.at[0, pl.ds(0, steps_down)], w_send.at[1])
        take(rs_snd.at[1, pl.ds(0, steps_down)], rs_send.at[1])
    take(rs_snd.at[0, pl.ds(0, steps_up)], rs_send.at[0])
    take(weights.at[pl.ds(0, nx - 1), pl.ds(0, nz - 1)], x_send.at[0])
    take(cot_far.at[pl.ds(0, nz - 1)], a_send.at[0])
    take(far.at[0, pl.ds(0, nz - 1)], a_send.at[1])
    take(out_snd.at[pl.ds(0, nz - 1)], a_send.at[2])
    take(upper.at[0, pl.ds(0, nz - 1)], a_send.at[3])
    take(lp_snd.at[pl.ds(0, nz - 1)], low_send.at[0])
    take(lb_rcv.at[pl.ds(0, ROWS - 1)], low_send.at[1])
    take(db_rcv.at[pl.ds(0, ROWS - 1)], low_send.at[2])
    take(dl_all.at[pl.ds(0, nz - 1)], low_send.at[3])
    take(grad_snd.at[pl.ds(0, FAR - 1)], g_send.at[0])
    take(fin_rcv.at[pl.ds(0, nx - 1)], g_send.at[1])
    take(sg_rcv.at[pl.ds(0, nx - 1)], s_send.at[0])
    take(gl_rcv.at[pl.ds(0, nx - 1)], s_send.at[1])


def per_device(nx, nz, acts, diag, cross, low_in, low_out, cot):
    tokens = acts.shape[0]
    scale = float(tokens * nx) ** (-0.5)
    rank = low_in.shape[1]
    split = (2, nz, RANK, BLK)
    packed_w = jnp.concatenate(
        [diag[NEAR:], cross[NEAR:], low_out.reshape(FAR, rank // FAR, BLK)], axis=1
    )
    zero = jnp.zeros_like(low_in)
    lin2 = jnp.stack([jnp.concatenate([low_in, zero], 1), jnp.concatenate([zero, low_in], 1)])
    vm = pltpu.VMEM
    dma = pltpu.SemaphoreType.DMA
    far = (nz, 2, RANK, BLK)
    low = (RANK, BLK)
    scratch = [
        vm((NEAR, *split), BF), vm((NEAR, *split), BF), vm((FAR, *far), BF), vm(far, BF), vm(far, BF), vm(split, BF), vm((8, 128), BF), vm(split, BF),
        vm((FAR, nz, PIECE, BLK), BF), vm((FAR + 1, *far), BF), vm((FAR, nz, PIECE, BLK), BF), vm((nx, nz, PIECE, BLK), BF), vm((nz, PIECE, BLK), BF),
        vm((2, nz // 2, PIECE, BLK), BF), vm((2, nz // 2, PIECE, BLK), BF), vm((PIECE, BLK), BF), vm((nx, PIECE, BLK), BF),
        vm((2, *split), BF), vm((NEAR, *split), BF), vm((NEAR, *split), BF), vm((NEAR, 2 * BLK, BLK), BF), vm((nx, NEAR, 2 * BLK, BLK), BF), vm(low, BF), vm((nx, *low), BF),
        vm((nz, *low), BF), vm((nz, *low), BF), vm(low, F32), vm((ROWS, *low), F32), vm((BLK, RANK), BF), vm((BLK, RANK), F32), vm(low, F32), vm((ROWS, *low), F32), vm(low, BF), vm((nz, *low), BF),
        dma((NEAR,)), dma((NEAR, 4)), dma((NEAR,)), dma((NEAR, 4)), dma((2,)), dma((nz,)), dma((1,)), dma((FAR, nz)),
        dma((4,)), dma((4,)), dma((4,)), dma((4,)), dma((2,)), dma((2 * nx,)), dma((2,)), dma((2, nz // 2)), dma((2,)), dma((NEAR + 1, nx)),
    ]
    whole = pl.BlockSpec(memory_space=pltpu.VMEM)
    out, gacts, gdiag, gcross, glin, glout = pl.pallas_call(
        functools.partial(kernel, nx, nz, scale),
        out_shape=(
            jax.ShapeDtypeStruct(split, BF),
            jax.ShapeDtypeStruct(split, BF),
            jax.ShapeDtypeStruct(diag.shape, F32),
            jax.ShapeDtypeStruct(cross.shape, F32),
            jax.ShapeDtypeStruct(low, F32),
            jax.ShapeDtypeStruct((FAR, RANK // FAR, BLK), F32),
        ),
        in_specs=[whole] * 6,
        out_specs=(whole,) * 6,
        scratch_shapes=scratch,
        compiler_params=pltpu.CompilerParams(
            collective_id=0, has_side_effects=True, vmem_limit_bytes=60 << 20
        ),
    )(acts.reshape(split), cot.reshape(split), diag, cross, packed_w, lin2)
    return (
        out.reshape(acts.shape), gacts.reshape(acts.shape), gdiag, gcross, glin.T, glout.reshape(low_out.shape),
    )


def solution(mesh):
    nx = mesh.shape["dp"]
    nz = mesh.shape["mp"] // ROWS
    return jax.shard_map(
        functools.partial(per_device, nx, nz),
        mesh=mesh,
        in_specs=(
            P("dp", "mp"), P(None, "mp", None), P(None, "mp", None),
            P("mp", None), P(None, "mp"), P("dp", "mp"),
        ),
        out_specs=(
            P("dp", "mp"), P("dp", "mp"), P(None, "mp", None),
            P(None, "mp", None), P("mp", None), P(None, "mp"),
        ),
        check_vma=False,
    )
```

time: 1380 us -> 229 us (0.17)
  the two profiles are of different devices: /device:TPU:8 before, /device:TPU:4 now
where the time goes in v2:
time: 229 us; the launch traced here: 228 us
  Pallas kernels  218 us (95%)
  local copies, waits for them, and re-layouts  8.37 us (4%)
    pallas_call x1, Pallas kernels, per_device(): pl.pallas_call(functools.partial(kernel, nx, nz, scale), out_shape=(jax.S...  218 us
    unnamed x19, local copies, waits for them, and re-layouts  8.01 us

profile of v2, /device:TPU:4, one launch (start us, length us, event | category | flops | bytes accessed | tf_op | source)
XLA Modules:
  0.0 228.1 jit_solution(51003084089184360)
XLA Ops:
  0.6 0.8 copy.12
  1.5 0.1 pad_bitcast_fusion.1
  1.5 0.6 pad_maximum_fusion.1.lin2
  2.2 0.0 copy-start.5
  2.2 0.0 slice-start
  2.2 0.0 slice-start.1
  2.2 0.7 copy-done.5
  2.9 0.2 slice-done
  3.1 0.1 slice-done.1
  3.2 0.7 pad_maximum_fusion.packed_w
  3.9 217.7 %shard_map.109 = (bf16[2,16,64,128]{3,2,1,0:T(8,128)(2,1)}, bf16[2,16,64,128]{3,2,1,0:T(8,128)(2,1)}, f32[7,128,128]{2,1,0:T(8,128)}, f32[7,128,128]{2,1,0:T(8,1...) custom-call(bf16[2,16,64,128]{3,2,1,0:T(8,128)(2,1)} %bitcast.11, bf16[2,16,64,128]{3,2,1,0:T(8,128)(2,1)} %bitcast.12, ...), custom_call_target="tpu_custom_call" | custom-call | tf_op jit(solution)/shard_map/pallas_call | solution.py:469
  221.6 0.0 copy-start
  221.6 1.9 copy.20
  223.6 0.0 copy-done
  223.6 0.0 copy-start.2
  223.6 0.8 copy.21
  224.4 0.4 copy-done.2
  224.8 0.0 copy-start.1
  224.8 0.8 copy.22
  225.5 0.4 copy-done.1
  226.0 0.0 copy-start.4
  226.0 0.8 copy.23
  226.7 0.0 copy-done.4
  226.7 0.0 copy-start.3
  226.7 0.6 copy.24
  227.3 0.2 copy-done.3
  227.5 0.6 copy.25
Async XLA Ops:
  2.2 0.7 copy-start.5
  2.2 0.9 slice-start
  2.2 1.0 slice-start.1
  221.6 1.9 copy-start
  223.6 1.2 copy-start.2
  224.8 1.2 copy-start.1
  226.0 0.8 copy-start.4
  226.7 0.8 copy-start.3

commit v3 on v2

--- a/solution.py
+++ b/solution.py
@@ -38,12 +38,12 @@
     nx, nz, scale,
     acts, cot, diag, cross, packed_w, lin2,
     out, gacts, gdiag, gcross, glin, glout,
-    near_in, near_z, far, cot_far, out_snd, out_rcv, d_snd, d_rcv,
-    weights, upper, grad_snd, grad_rcv, red, rs_snd, rs_rcv, fin_snd, fin_rcv,
+    near_in, near_z, far, cot_far, out_snd, out_rcv, d_rcv,
+    weights, upper, grad_snd, grad_rcv, rs_snd, rs_rcv, fin_snd, fin_rcv,
     near_dz, q_snd, q_rcv, sg_snd, sg_rcv, gl_snd, gl_rcv,
     lp_snd, lp_rcv, lb_snd, lb_rcv, low_u, dacc, db_snd, db_rcv, dl_snd, dl_all,
     f_send, f_recv, b_send, b_recv, w_send, w_recv, x_send, x_recv,
-    a_send, a_recv, low_send, low_recv, g_send, g_recv, rs_send, rs_recv, s_send, s_recv,
+    a_send, a_recv, low_send, low_recv, g_send, g_recv, fin_recv, rs_send, rs_recv, s_send, s_recv,
 ):
     x = lax.axis_index("dp")
     n = lax.axis_index("mp")
@@ -123,6 +123,15 @@
             one((z + k) % nz)
 
     w_pass(0)
+
+    def some(first, stop, fn):
+        def one(k, _):
+            fn((z + k) % nz)
+            return 0
+        if first < min(stop, nz):
+            lax.fori_loop(first, min(stop, nz), one, 0)
+
+    some(1, nz, lambda zz: send(cot.at[:, zz], cot_far.at[z], a_send.at[0], a_recv.at[0], at_z(zz)))
     for q in range(FAR):
         weights[q, z] = packed_w[q]
 
@@ -137,8 +146,16 @@
             return 0
         lax.fori_loop(1, count, one, 0)
 
-    far_all(nz, lambda zz: send(lp_snd.at[zz], lp_rcv.at[z], low_send.at[0], low_recv.at[0], at_z(zz)))
     lp_rcv[z] = lp_snd[z]
+    cot_far[z] = cot[:, z]
+
+    def low_some(first, stop):
+        some(first, stop, lambda zz: send(lp_snd.at[zz], lp_rcv.at[z], low_send.at[0], low_recv.at[0], at_z(zz)))
+
+    def ring(k):
+        if k <= steps_up:
+            w_take(k)
+            w_pass(k)
 
     def near_forward(section, src, dst, after):
         both = jnp.concatenate([diag[section], cross[section]], axis=0)
@@ -150,22 +167,30 @@
 
     def after0(j):
         near_send(near_z.at[0], near_in.at[1], j, 1, f_send.at[1], f_recv.at[1, j])
+        if j == 3:
+            ring(1)
 
     near_forward(0, acts, near_z.at[0], after0)
-
-    far_all(nz, lambda zz: send(cot.at[:, zz], cot_far.at[z], a_send.at[0], a_recv.at[0], at_z(zz)))
-    cot_far[z] = cot[:, z]
-
-    def ring(k):
-        if k <= steps_up:
-            w_take(k)
-            w_pass(k)
 
     def after1(j):
         near_send(near_z.at[1], near_in.at[2], j, 2, f_send.at[2], f_recv.at[2, j])
-        ring(1 + j)
+        if j % 2:
+            ring(2 + j // 2)
 
     near_forward(1, near_z.at[0], near_z.at[1], after1)
+
+    def after2(j):
+        if j % 2:
+            c = j // 2
+            far_all(nz, lambda zz: send(near_z.at[2, c, zz], far.at[0, z, c], a_send.at[1], a_recv.at[1], at_z(zz)))
+            far[0, z, c] = near_z[2, c, z]
+        if j < 3:
+            ring(4 + j)
+            low_some(1 + 5 * j, 6 + 5 * j)
+
+    near_forward(2, near_z.at[1], near_z.at[2], after2)
+    for k in range(7, steps_up + 1):
+        ring(k)
 
     take(lp_rcv.at[pl.ds(0, nz - 1)], low_recv.at[0])
     total = lp_rcv[0].astype(F32)
@@ -181,24 +206,6 @@
 
     plane_all(lb_snd, lb_rcv, 1)
     lb_rcv[r] = lb_snd[...]
-
-    def after2(j):
-        if j % 2:
-            c = j // 2
-            far_all(nz, lambda zz: send(near_z.at[2, c, zz], far.at[0, z, c], a_send.at[1], a_recv.at[1], at_z(zz)))
-            far[0, z, c] = near_z[2, c, z]
-        ring(5 + j)
-
-    near_forward(2, near_z.at[1], near_z.at[2], after2)
-    for k in range(9, steps_up + 1):
-        ring(k)
-
-    take(lb_rcv.at[pl.ds(0, ROWS - 1)], low_recv.at[1])
-    total = lb_rcv[0]
-    for rr in range(1, ROWS):
-        total = total + lb_rcv[rr]
-    low_u[0:RANK] = total[:, :RANK].astype(BF)
-    low_u[RANK:BLK] = total[:, RANK:].astype(BF)
 
     take(far.at[0, pl.ds(0, nz - 1)], a_recv.at[1])
 
@@ -226,6 +233,12 @@
             return 0
         lax.fori_loop(0, nz, forward, 0, unroll=2)
 
+    take(lb_rcv.at[pl.ds(0, ROWS - 1)], low_recv.at[1])
+    total = lb_rcv[0]
+    for rr in range(1, ROWS):
+        total = total + lb_rcv[rr]
+    low_u[0:RANK] = total[:, :RANK].astype(BF)
+    low_u[RANK:BLK] = total[:, RANK:].astype(BF)
     weights_ready(FAR - 1)
     take(cot_far.at[pl.ds(0, nz - 1)], a_recv.at[0])
     dacc[...] = jnp.zeros_like(dacc)
@@ -247,7 +260,7 @@
 
         @pl.when(b != z)
         def _():
-            send(out_snd.at[b], out_rcv.at[:, z], a_send.at[2], a_recv.at[2], at_z(b))
+            send(out_snd.at[b, 0], out_rcv.at[0, z], a_send.at[2], a_recv.at[2], at_z(b))
         return 0
 
     lax.fori_loop(1, nz + 1, last, 0)
@@ -272,13 +285,24 @@
             if q == 0:
                 @pl.when(b != z)
                 def _():
-                    send(upper.at[0, b], d_rcv.at[:, z], a_send.at[3], a_recv.at[3], at_z(b))
+                    send(upper.at[0, b, 0], d_rcv.at[0, z], a_send.at[3], a_recv.at[3], at_z(b))
             return 0
         lax.fori_loop(1, nz + 1, backward, 0, unroll=2 if q else 1)
 
         @pl.when(x != q)
         def _():
-            send(grad_snd.at[q], grad_rcv.at[x], g_send.at[0], g_recv.at[x], (q, n))
+            def piece(b):
+                send(grad_snd.at[q, b], grad_rcv.at[x, b], g_send.at[0], g_recv.at[x, b], (q, n))
+
+            def both_ways(i, _):
+                piece((z + steps_up - i) % nz)
+
+                @pl.when(i < steps_down)
+                def _():
+                    piece((z + nz - steps_down + i) % nz)
+                return 0
+            lax.fori_loop(0, steps_up, both_ways, 0)
+            piece(z)
 
         if q == FAR - 1:
             take(db_rcv.at[pl.ds(0, ROWS - 1)], low_recv.at[2])
@@ -286,36 +310,34 @@
             for rr in range(1, ROWS):
                 total = total + db_rcv[rr]
             dl_snd[...] = total.astype(BF)
-            far_all(nz, lambda zz: send(dl_snd, dl_all.at[z], low_send.at[3], low_recv.at[3], at_z(zz)))
             dl_all[z] = dl_snd[...]
     d_rcv[:, z] = upper[0, z]
-
-    def red_all():
+    far_all(nz, lambda zz: send(upper.at[0, zz, 1], d_rcv.at[1, z], a_send.at[4], a_recv.at[4], at_z(zz)))
+
+    def low_back_some(first, stop):
+        some(first, stop, lambda zz: send(dl_snd, dl_all.at[z], low_send.at[3], low_recv.at[3], at_z(zz)))
+
+    def out_some(first, stop):
+        some(first, stop, lambda zz: send(out_snd.at[zz, 1], out_rcv.at[1, z], a_send.at[5], a_recv.at[5], at_z(zz)))
+
+    def red(b):
+        total = grad_snd[x, b].astype(F32)
         for d in range(1, nx):
-            take(grad_rcv.at[(x + d) % nx], g_recv.at[(x + d) % nx])
-
-        def one(b, _):
-            total = grad_snd[x, b].astype(F32)
-            for d in range(1, nx):
-                total = total + grad_rcv[(x + d) % nx, b].astype(F32)
-            red[b] = total.astype(BF)
-            return 0
-        lax.fori_loop(0, nz, one, 0)
+            take(grad_rcv.at[(x + d) % nx, b], g_recv.at[(x + d) % nx, b])
+            total = total + grad_rcv[(x + d) % nx, b].astype(F32)
+        return total
 
     def rs_step(k):
         up, down = (z + steps_up + 1 - k) % nz, (z + nz - (steps_down + 1 - k)) % nz
         for direction, target, where, count in ((0, up, (z + 1) % nz, steps_up), (1, down, (z + nz - 1) % nz, steps_down)):
             if k > count:
                 continue
-            if k == 1:
-                src = red.at[target]
-            else:
+            total = red(target)
+            if k > 1:
                 take(rs_rcv.at[direction, k - 2], rs_recv.at[direction, k - 2])
-                rs_snd[direction, k - 1] = (rs_rcv[direction, k - 2].astype(F32) + red[target].astype(F32)).astype(BF)
-                src = rs_snd.at[direction, k - 1]
-            send(src, rs_rcv.at[direction, k - 1], rs_send.at[direction], rs_recv.at[direction, k - 1], at_z(where))
-
-    take(d_rcv.at[:, pl.ds(0, nz - 1)], a_recv.at[3])
+                total = total + rs_rcv[direction, k - 2].astype(F32)
+            rs_snd[direction, k - 1] = total.astype(BF)
+            send(rs_snd.at[direction, k - 1], rs_rcv.at[direction, k - 1], rs_send.at[direction], rs_recv.at[direction, k - 1], at_z(where))
 
     def near_q(section, src, j):
         q_snd[section, j // 2, pl.ds((j % 2) * hz, hz)] = mm_nt(load(src, j), cross[section]).astype(BF).reshape(hz, RANK, BLK)
@@ -334,29 +356,38 @@
         lax.fori_loop(1, nx, other, 0)
         sg_rcv[x, section] = sg_snd[section]
 
+    rs_step(1)
+    low_back_some(1, 6)
     for j in range(4):
+        if j % 2 == 0:
+            take(d_rcv.at[j // 2, pl.ds(0, nz - 1)], a_recv.at[3 + j // 2])
         near_q(2, d_rcv, j)
+    rs_step(2)
+    low_back_some(6, 11)
     near_grad(2, near_z.at[1], d_rcv)
-    red_all()
-    rs_step(1)
 
     def near_back(section, src, j):
         take(chunk(q_rcv.at[section], j), b_recv.at[section, j])
         return mm_nt(load(src, j), diag[section]) + load(q_rcv.at[section], j).astype(F32)
 
-    for section, src, state in ((2, d_rcv, None), (1, near_dz.at[1], near_z.at[0])):
+    for section, src in ((2, d_rcv), (1, near_dz.at[1])):
         dst = near_dz.at[section - 1]
         for j in range(4):
             back = near_back(section, src, j)
             dst[j // 2, pl.ds((j % 2) * hz, hz)] = back.astype(BF).reshape(hz, RANK, BLK)
             near_q(section - 1, dst, j)
+            if section == 2 and j % 2:
+                rs_step(3 + j // 2)
+                if j == 1:
+                    low_back_some(11, nz)
+                else:
+                    out_some(1, 5)
+            if section == 1 and j < 3:
+                rs_step(5 + j)
+                out_some(5 + 4 * j, 9 + 4 * j)
         if section == 2:
             near_grad(1, near_z.at[0], near_dz.at[1])
-        else:
-            near_grad(0, acts, near_dz.at[0])
-        for k in range(2 + 3 * (2 - section), 5 + 3 * (2 - section)):
-            if k <= steps_up:
-                rs_step(k)
+    near_grad(0, acts, near_dz.at[0])
 
     take(dl_all.at[pl.ds(0, nz - 1)], low_recv.at[3])
     total = None
@@ -382,18 +413,19 @@
         gacts[j // 2, zs] = back.astype(BF).reshape(hz, RANK, BLK)
 
     take(rs_rcv.at[0, steps_up - 1], rs_recv.at[0, steps_up - 1])
-    total = red[z].astype(F32) + rs_rcv[0, steps_up - 1].astype(F32)
+    total = red(z) + rs_rcv[0, steps_up - 1].astype(F32)
     if steps_down:
         take(rs_rcv.at[1, steps_down - 1], rs_recv.at[1, steps_down - 1])
         total = total + rs_rcv[1, steps_down - 1].astype(F32)
     fin_snd[...] = total.astype(BF)
     def final(d, _):
-        send(fin_snd, fin_rcv.at[x], g_send.at[1], g_recv.at[nx + x], at_x((x + d) % nx))
+        send(fin_snd, fin_rcv.at[x], g_send.at[1], fin_recv.at[x], at_x((x + d) % nx))
         return 0
     lax.fori_loop(1, nx, final, 0)
     fin_rcv[x] = fin_snd[...]
 
-    take(out_rcv.at[:, pl.ds(0, nz - 1)], a_recv.at[2])
+    take(out_rcv.at[0, pl.ds(0, nz - 1)], a_recv.at[2])
+    take(out_rcv.at[1, pl.ds(0, nz - 1)], a_recv.at[5])
     out[...] = out_rcv[...]
 
     for section in range(NEAR):
@@ -412,7 +444,7 @@
         total = total + gl_rcv[xx].astype(F32)
     glin[...] = total * scale
     for d in range(1, nx):
-        take(fin_rcv.at[(x + d) % nx], g_recv.at[nx + (x + d) % nx])
+        take(fin_rcv.at[(x + d) % nx], fin_recv.at[(x + d) % nx])
     for q in range(FAR):
         total = fin_rcv[q].astype(F32) * scale
         gdiag[NEAR + q] = total[0:BLK]
@@ -430,8 +462,9 @@
     take(weights.at[pl.ds(0, nx - 1), pl.ds(0, nz - 1)], x_send.at[0])
     take(cot_far.at[pl.ds(0, nz - 1)], a_send.at[0])
     take(far.at[0, pl.ds(0, nz - 1)], a_send.at[1])
-    take(out_snd.at[pl.ds(0, nz - 1)], a_send.at[2])
-    take(upper.at[0, pl.ds(0, nz - 1)], a_send.at[3])
+    for c in range(2):
+        take(out_rcv.at[c, pl.ds(0, nz - 1)], a_send.at[2 + 3 * c])
+        take(d_rcv.at[c, pl.ds(0, nz - 1)], a_send.at[3 + c])
     take(lp_snd.at[pl.ds(0, nz - 1)], low_send.at[0])
     take(lb_rcv.at[pl.ds(0, ROWS - 1)], low_send.at[1])
     take(db_rcv.at[pl.ds(0, ROWS - 1)], low_send.at[2])
@@ -457,13 +490,13 @@
     far = (nz, 2, RANK, BLK)
     low = (RANK, BLK)
     scratch = [
-        vm((NEAR, *split), BF), vm((NEAR, *split), BF), vm((FAR, *far), BF), vm(far, BF), vm(far, BF), vm(split, BF), vm((8, 128), BF), vm(split, BF),
-        vm((FAR, nz, PIECE, BLK), BF), vm((FAR + 1, *far), BF), vm((FAR, nz, PIECE, BLK), BF), vm((nx, nz, PIECE, BLK), BF), vm((nz, PIECE, BLK), BF),
+        vm((NEAR, *split), BF), vm((NEAR, *split), BF), vm((FAR, *far), BF), vm(far, BF), vm(far, BF), vm(split, BF), vm(split, BF),
+        vm((FAR, nz, PIECE, BLK), BF), vm((FAR + 1, *far), BF), vm((FAR, nz, PIECE, BLK), BF), vm((nx, nz, PIECE, BLK), BF),
         vm((2, nz // 2, PIECE, BLK), BF), vm((2, nz // 2, PIECE, BLK), BF), vm((PIECE, BLK), BF), vm((nx, PIECE, BLK), BF),
         vm((2, *split), BF), vm((NEAR, *split), BF), vm((NEAR, *split), BF), vm((NEAR, 2 * BLK, BLK), BF), vm((nx, NEAR, 2 * BLK, BLK), BF), vm(low, BF), vm((nx, *low), BF),
         vm((nz, *low), BF), vm((nz, *low), BF), vm(low, F32), vm((ROWS, *low), F32), vm((BLK, RANK), BF), vm((BLK, RANK), F32), vm(low, F32), vm((ROWS, *low), F32), vm(low, BF), vm((nz, *low), BF),
         dma((NEAR,)), dma((NEAR, 4)), dma((NEAR,)), dma((NEAR, 4)), dma((2,)), dma((nz,)), dma((1,)), dma((FAR, nz)),
-        dma((4,)), dma((4,)), dma((4,)), dma((4,)), dma((2,)), dma((2 * nx,)), dma((2,)), dma((2, nz // 2)), dma((2,)), dma((NEAR + 1, nx)),
+        dma((6,)), dma((6,)), dma((4,)), dma((4,)), dma((2,)), dma((nx, nz)), dma((nx,)), dma((2,)), dma((2, nz // 2)), dma((2,)), dma((NEAR + 1, nx)),
     ]
     whole = pl.BlockSpec(memory_space=pltpu.VMEM)
     out, gacts, gdiag, gcross, glin, glout = pl.pallas_call(

time: 229 us -> 208 us (0.908)
  Pallas kernels: 218 us -> 197 us
    pallas_call x1, Pallas kernels: 218 us -> 197 us  [per_device(): pl.pallas_call(functools.partial(kernel, nx, nz, scale), out_shape=(jax.S...]
where the time goes in v3:
time: 208 us
  Pallas kernels  197 us (95%)
  local copies, waits for them, and re-layouts  8.37 us (4%)
    pallas_call x1, Pallas kernels, per_device(): pl.pallas_call(functools.partial(kernel, nx, nz, scale), out_shape=(jax.S...  197 us
    unnamed x19, local copies, waits for them, and re-layouts  8.01 us

profile of v3, /device:TPU:4, one launch (start us, length us, event | category | flops | bytes accessed | tf_op | source)
XLA Modules:
  0.0 207.7 jit_solution(11984131070134138165)
XLA Ops:
  0.6 0.8 copy.12
  1.5 0.1 pad_bitcast_fusion.1
  1.5 0.6 pad_maximum_fusion.1.lin2
  2.2 0.0 copy-start.5
  2.2 0.0 slice-start
  2.2 0.0 slice-start.1
  2.2 0.7 copy-done.5
  2.9 0.2 slice-done
  3.1 0.1 slice-done.1
  3.2 0.7 pad_maximum_fusion.packed_w
  3.9 197.3 %shard_map.109 = (bf16[2,16,64,128]{3,2,1,0:T(8,128)(2,1)}, bf16[2,16,64,128]{3,2,1,0:T(8,128)(2,1)}, f32[7,128,128]{2,1,0:T(8,128)}, f32[7,128,128]{2,1,0:T(8,1...) custom-call(bf16[2,16,64,128]{3,2,1,0:T(8,128)(2,1)} %bitcast.11, bf16[2,16,64,128]{3,2,1,0:T(8,128)(2,1)} %bitcast.12, ...), custom_call_target="tpu_custom_call" | custom-call | tf_op jit(solution)/shard_map/pallas_call | solution.py:502
  201.3 0.0 copy-start
  201.3 1.9 copy.20
  203.2 0.0 copy-done
  203.2 0.0 copy-start.2
  203.2 0.8 copy.21
  204.0 0.4 copy-done.2
  204.4 0.0 copy-start.1
  204.4 0.8 copy.22
  205.2 0.4 copy-done.1
  205.6 0.0 copy-start.4
  205.6 0.8 copy.23
  206.4 0.0 copy-done.4
  206.4 0.0 copy-start.3
  206.4 0.6 copy.24
  207.0 0.2 copy-done.3
  207.1 0.6 copy.25
Async XLA Ops:
  2.2 0.7 copy-start.5
  2.2 0.9 slice-start
  2.2 1.0 slice-start.1
  201.3 1.9 copy-start
  203.2 1.2 copy-start.2
  204.4 1.2 copy-start.1
  205.6 0.8 copy-start.4
  206.4 0.8 copy-start.3
